TPU v7x, 128 devices: a whole 4x4x4 slice. The times are simulated.
128 devices in a mesh: group: 4 (over x), bulk: 32 (over z, y, core).
Axes of the slice: x: 4, y: 4, z: 4, core: 2. Of those that a mesh axis runs over, the one named last changes fastest.
Arguments:
- rhs: float32 [512, 64, 128], P(('group', 'bulk')), may hold values from -90 to 90, as said below
- diag_tiles: float32 [512, 128, 128], P(('group', 'bulk')), may hold values from -0.06 to 0.06
- offdiag_blocks: float32 [512, 11, 128, 128], P(('group', 'bulk')), may hold values from -0.026 to 0.026
- coupling: float32 [256, 4, 128, 128], P(('group', 'bulk')), may hold values from -0.05 to 0.05, as said below
- col_index: int32 [512, 11], replicated, may hold values from 0 to 511, as said below
- load: int32 [512], replicated, may hold values from 3 to 11
- new_slot: int32 [512], replicated, may hold values from 0 to 511, as said below
Outputs:
- solution_out: float32 [512, 64, 128], P(('group', 'bulk'))
- residual_out: float32 [512, 64, 128], P(('group', 'bulk'))
Inputs may be any that keep to these rules, and one draw needn't show every extreme that they name: `rhs`: made of random entries times scales of the rows and of the columns. `coupling`: entry [d * 2 + k, h] is the transpose of entry [(h * 32 + d % 32) * 2 + k, d // 32]. `col_index`: for each part g and each tile position t, the column t of the 128 block rows of part g is a permutation of that part's slots g * 128 to (g + 1) * 128 - 1. Of the 44 entries of the 4 block rows of one device (slots d * 4 to (d + 1) * 4 - 1), at most 2 name slots of any one device, and exactly 2 name slots of some device. `new_slot`: A permutation. On every device exactly one block row moves, from a slot k with 2 <= k % 4; it stays in its part, goes from owner b to owner b XOR m, where m (1 to 31) is one number for the whole part, and takes the slot that the moving row of that device leaves.
All inputs are finite; a program needn't handle non-finite values.
Results may differ from a plain program's by a relative error of at most 0.0003.
Values sent between devices are 32-bit elements; how exact they have to be, the bound alone decides.
A program may use at most 64 MiB of HBM per device.

v0:
```python
import jax
import jax.numpy as jnp
from jax import lax
from jax.sharding import PartitionSpec as P

highest = lax.Precision.HIGHEST
diagonal_shift = 4.0


def chol_apply(matrix, right):
    factor = jnp.linalg.cholesky(matrix)
    middle = lax.linalg.triangular_solve(factor, right, left_side=True, lower=True)
    return lax.linalg.triangular_solve(factor, middle, left_side=True, lower=True, transpose_a=True)


def gram(left, right):
    return jnp.einsum("snt,smt->nm", left, right, precision=highest)


def sym(m):
    return 0.5 * (m + m.T)


def mm(a, b):
    return jnp.dot(a, b, precision=highest)


def off_part(vectors, diag, masked, column_ids, coupling):
    boundary_rows = coupling.shape[0]
    part_count = coupling.shape[1]
    border = lax.all_gather(vectors[:boundary_rows], "group", axis=0, tiled=True)
    own = jnp.einsum("rnj,rij->rni", vectors, diag, precision=highest)
    returned = jnp.einsum("rni,rkij->rknj", vectors, masked, precision=highest)
    panel = lax.all_gather(vectors, "bulk", axis=0, tiled=True)
    picked = panel[column_ids]
    own = own + jnp.einsum("rknj,rkij->rni", picked, masked, precision=highest)
    border = border.reshape((part_count, boundary_rows) + vectors.shape[1:])
    crossed = jnp.einsum("khij,hknj->kni", coupling, border, precision=highest)
    return (own.at[:boundary_rows].add(crossed), returned.reshape((-1,) + vectors.shape[1:]), panel)


def coefficients(n0, n1, n2, n3):
    n = n0.shape[0]
    eye = jnp.eye(n, dtype=n0.dtype)
    n0, n1, n2, n3 = (sym(n0), sym(n1), sym(n2), sym(n3))
    delta = chol_apply(diagonal_shift * n0 + n1, n1)
    alpha = (eye - delta) / diagonal_shift
    b = -alpha
    cross = mm(delta.T, mm(n1, b))
    gram_new = sym(mm(delta.T, mm(n0, delta)) + cross + cross.T + mm(b.T, mm(n2, b)))
    beta = chol_apply(n0, gram_new)
    a = delta + beta
    c1 = mm(a.T, mm(n1, b))
    c2 = mm(a.T, mm(n2, b))
    pp = mm(a.T, mm(n0, a)) + c1 + c1.T + mm(b.T, mm(n2, b))
    pep = mm(a.T, mm(n1, a)) + c2 + c2.T + mm(b.T, mm(n3, b))
    alpha2 = chol_apply(sym(diagonal_shift * pp + pep), gram_new)
    ba = mm(b, alpha2)
    aa = mm(a, alpha2)
    sol = (alpha + aa, ba)
    res = (delta - diagonal_shift * aa, b - diagonal_shift * ba - aa, -ba)
    return (sol, res)


def local(rhs, diag_tiles, offdiag_blocks, coupling, col_index, load, new_slot):
    row_count = rhs.shape[0]
    off_count = offdiag_blocks.shape[1]
    bulk_count = lax.axis_size("bulk")
    group_rows = row_count * bulk_count
    group_base = lax.axis_index("group") * group_rows
    first = lax.axis_index("bulk") * row_count
    cols = lax.dynamic_slice_in_dim(col_index, group_base, group_rows) - group_base
    moved = lax.dynamic_slice_in_dim(new_slot, group_base, group_rows) - group_base
    loads = lax.dynamic_slice_in_dim(load, group_base + first, row_count)
    my_cols = lax.dynamic_slice_in_dim(cols, first, row_count)
    my_new = lax.dynamic_slice_in_dim(moved, first, row_count)
    tile_ids = jnp.arange(off_count, dtype=jnp.int32)
    mask = (tile_ids[None, :] < loads[:, None]).astype(jnp.float32)
    masked = offdiag_blocks * mask[:, :, None, None]
    u0 = rhs
    own, returned, panel0 = off_part(u0, diag_tiles, masked, my_cols, coupling)
    buffer = jax.ops.segment_sum(returned, my_cols.reshape(-1), num_segments=group_rows)
    u1 = own + lax.psum_scatter(buffer, "bulk", scatter_dimension=0, tiled=True)
    own, returned, panel1 = off_part(u1, diag_tiles, masked, my_cols, coupling)
    ids = jnp.concatenate([moved[my_cols.reshape(-1)], my_new])
    buffer = jax.ops.segment_sum(jnp.concatenate([returned, own]), ids, num_segments=group_rows)
    u2 = lax.psum_scatter(buffer, "bulk", scatter_dimension=0, tiled=True)
    inverse = jnp.zeros_like(moved).at[moved].set(jnp.arange(group_rows, dtype=jnp.int32))
    mine = lax.dynamic_slice_in_dim(inverse, first, row_count)
    v0, v1 = (panel0[mine], panel1[mine])
    grams = jnp.stack([gram(v0, v0), gram(v0, v1), gram(v1, v1), gram(v1, u2)])
    grams = lax.psum(grams, ("group", "bulk"))
    sol, res = coefficients(grams[0], grams[1], grams[2], grams[3])
    basis = jnp.concatenate([v0, v1, u2], axis=1)
    zero = jnp.zeros_like(sol[0])
    weights = jnp.concatenate(
        [jnp.concatenate(sol + (zero,), axis=0), jnp.concatenate(res, axis=0)], axis=1
    )
    out = jnp.einsum("mn,smt->snt", weights, basis, precision=highest)
    n = rhs.shape[1]
    return (out[:, :n], out[:, n:])


def solution(mesh):
    return jax.shard_map(
        local,
        mesh=mesh,
        in_specs=(
            P(("group", "bulk"), None, None),
            P(("group", "bulk"), None, None),
            P(("group", "bulk"), None, None, None),
            P(("group", "bulk"), None, None, None),
            P(),
            P(),
            P(),
        ),
        out_specs=(P(("group", "bulk"), None, None), P(("group", "bulk"), None, None)),
        check_vma=False,
    )
```

profile of v0, /device:TPU:1, one launch (start us, length us, event | category | flops | bytes accessed | tf_op | source)
XLA Modules:
  0.0 494.6 jit_solution(10182201475086260046)
XLA Ops:
  9.8 3.8 fusion.4
  13.5 2.5 broadcast.140.clone
  16.0 6.9 %scatter_fusion = f32[128,64,128]{2,1,0:T(8,128)} fusion(f32[128,64,128]{2,1,0:T(8,128)} %broadcast.140.clone, s32[44]{0:T(128)S(1)} %reshape.206, f32[44,64,128]{2,1,0:T(8,128)S(1)} %bitcast.248), kind=kCustom, calls=%fused_computation.6 | custom fusion | flops 360448 | bytes 4325552 | tf_op jit(solution)/shard_map/scatter-add | solution.py:82
  25.9 12.7 %all_gather.13 = f32[8,64,128]{2,1,0:T(8,128)} all-gather(f32[2,64,128]{2,1,0:T(8,128)} %slice.81), channel_id=1, replica_groups=mesh['group'=4,'bulk'=32] {'group'}, dimensions={0}, use_global_device_ids=true | all-gather | bytes 327680 | tf_op jit(solution)/shard_map/all_gather | solution.py:31
  38.5 21.5 %all-gather.3.cloned.1.call-done = f32[128,64,128]{2,1,0:T(8,128)} async-done(((f32[4,64,128]{2,1,0:T(8,128)}), f32[128,64,128]{2,1,0:T(8,128)}) %all-gather.3.cloned.1.call-update) | async-done | bytes 4194320 | tf_op jit(solution)/shard_map/all_gather | solution.py:34
  60.1 4.0 gather_fusion.1
  64.1 4.8 fusion.12
  68.9 1.3 convolution_add_fusion.1
  70.2 2.1 fusion.21
  72.4 71.0 %reduce-scatter.3.cloned.1.call-done = f32[4,64,128]{2,1,0:T(8,128)} async-done(((f32[128,64,128]{2,1,0:T(8,128)}), f32[4,64,128]{2,1,0:T(8,128)}) %reduce-scatter.3.cloned.1.call-update) | async-done | bytes 131088 | tf_op jit(solution)/shard_map/reduce_scatter | solution.py:83
  143.4 1.6 add.181
  147.7 10.6 %all_gather.15 = f32[8,64,128]{2,1,0:T(8,128)} all-gather(f32[2,64,128]{2,1,0:T(8,128)S(1)} %slice.102), channel_id=1, replica_groups=mesh['group'=4,'bulk'=32] {'group'}, dimensions={0}, use_global_device_ids=true | all-gather | bytes 327680 | tf_op jit(solution)/shard_map/all_gather | solution.py:31
  158.3 4.1 fusion.2
  162.4 31.4 %all-gather.5.cloned.1.call-done = f32[128,64,128]{2,1,0:T(8,128)} async-done(((f32[4,64,128]{2,1,0:T(8,128)}), f32[128,64,128]{2,1,0:T(8,128)}) %all-gather.5.cloned.1.call-update) | async-done | bytes 4194320 | tf_op jit(solution)/shard_map/all_gather | solution.py:34
  193.8 3.9 gather_fusion.4
  197.7 4.9 fusion.15
  204.1 2.5 broadcast.140
  206.6 6.9 %scatter_fusion.1 = f32[128,64,128]{2,1,0:T(8,128)} fusion(f32[128,64,128]{2,1,0:T(8,128)} %broadcast.140, s32[48]{0:T(128)S(1)} %pad_add_fusion, f32[48,64,128]{2,1,0:T(8,128)S(1)} %pad_maximum_fusion), kind=kCustom, calls=%fused_computation.7 | custom fusion | flops 393216 | bytes 4718784 | tf_op jit(solution)/shard_map/scatter-add | solution.py:86
  213.6 1.2 scatter_custom_fusion
  214.9 2.7 gather_fusion
  217.9 2.7 gather_fusion.2
  221.1 72.2 %reduce-scatter.5.cloned.1.call-done = f32[4,64,128]{2,1,0:T(8,128)} async-done(((f32[128,64,128]{2,1,0:T(8,128)}), f32[4,64,128]{2,1,0:T(8,128)}) %reduce-scatter.5.cloned.1.call-update) | async-done | bytes 131088 | tf_op jit(solution)/shard_map/reduce_scatter | solution.py:87
  293.4 1.2 convolution_bitcast_fusion.3
  295.2 146.3 %all-reduce.2.cloned.1.call-done = f32[4,64,64]{2,1,0:T(8,128)} async-done(((f32[4,64,64]{2,1,0:T(8,128)}), f32[4,64,64]{2,1,0:T(8,128)}) %all-reduce.2.cloned.1.call-update) | async-done | bytes 65552 | tf_op jit(solution)/shard_map/psum | solution.py:92
  443.6 5.9 %cholesky.59 = f32[64,64]{1,0:T(8,128)S(1)} custom-call(f32[64,64]{1,0:T(8,128)S(1)} %copy.82), custom_call_target="Cholesky" | custom-call | tf_op jit(solution)/shard_map/jit(cholesky)/cholesky | solution.py:11
  450.8 4.9 custom-call.13
  456.7 5.9 %cholesky.70 = f32[64,64]{1,0:T(8,128)S(1)} custom-call(f32[64,64]{1,0:T(8,128)S(1)} %copy.85), custom_call_target="Cholesky" | custom-call | tf_op jit(solution)/shard_map/jit(cholesky)/cholesky | solution.py:11
  463.9 4.9 custom-call.15
  468.8 1.0 fusion.67
  471.9 1.0 fusion.45
  473.9 5.8 %cholesky.81 = f32[64,64]{1,0:T(8,128)S(1)} custom-call(f32[64,64]{1,0:T(8,128)S(1)} %fusion.51), custom_call_target="Cholesky" | custom-call | tf_op jit(solution)/shard_map/jit(cholesky)/cholesky | solution.py:11
  481.1 4.9 custom-call.17
  (112 shorter events, 23.2 us)
Async XLA Ops:
  7.2 63.1 %copy-start = (f32[2,4,128,128]{3,2,1,0:T(8,128)S(1)}, f32[2,4,128,128]{3,2,1,0:T(8,128)}, u32[]{:S(2)}) copy-start(f32[2,4,128,128]{3,2,1,0:T(8,128)} %param.19) | copy-start | bytes 1572868
  7.2 52.9 %all-gather.3.cloned.1.call-start = ((), (), s32[]{:S(2)}) async-start(), calls=%async_computation.2 | async-start | bytes 4325376 | tf_op jit(solution)/shard_map/all_gather | solution.py:34
  7.9 135.5 %reduce-scatter.3.cloned.1.call-start = ((), (), s32[]{:S(2)}) async-start(), calls=%async_computation.3 | async-start | bytes 4325376 | tf_op jit(solution)/shard_map/reduce_scatter | solution.py:83
  22.9 0.9 copy-start.4
  22.9 41.2 %copy-start.1 = (f32[4,11,128,128]{3,2,1,0:T(8,128)S(1)}, f32[4,11,128,128]{3,2,1,0:T(8,128)}, u32[]{:S(2)}) copy-start(f32[4,11,128,128]{3,2,1,0:T(8,128)} %param.18) | copy-start | bytes 8650756
  22.9 170.9 %all-gather.5.cloned.1.call-start = ((), (), s32[]{:S(2)}) async-start(), calls=%async_computation.4 | async-start | bytes 4325376 | tf_op jit(solution)/shard_map/all_gather | solution.py:34
  64.1 4.8 copy-start.7
  64.1 6.1 %copy-start.6 = (f32[8,64,128]{2,1,0:T(8,128)S(1)}, f32[8,64,128]{2,1,0:T(8,128)}, u32[]{:S(2)}) copy-start(f32[8,64,128]{2,1,0:T(8,128)} %all_gather.13) | copy-start | bytes 786436
  145.0 148.3 %reduce-scatter.5.cloned.1.call-start = ((), (), s32[]{:S(2)}) async-start(), calls=%async_computation.5 | async-start | bytes 4325376 | tf_op jit(solution)/shard_map/reduce_scatter | solution.py:87
  197.7 4.9 copy-start.3
  197.7 4.9 %copy-start.8 = (f32[4,128,128]{2,1,0:T(8,128)S(1)}, f32[4,128,128]{2,1,0:T(8,128)}, u32[]{:S(2)}) copy-start(f32[4,128,128]{2,1,0:T(8,128)} %param.17) | copy-start | bytes 786436
  197.7 5.6 %copy-start.5 = (f32[8,64,128]{2,1,0:T(8,128)S(1)}, f32[8,64,128]{2,1,0:T(8,128)}, u32[]{:S(2)}) copy-start(f32[8,64,128]{2,1,0:T(8,128)} %all_gather.15) | copy-start | bytes 786436
  197.7 6.2 %copy-start.2 = (f32[4,11,128,64]{2,3,1,0:T(8,128)S(1)}, f32[4,11,128,64]{2,3,1,0:T(8,128)}, u32[]{:S(2)}) copy-start(f32[4,11,128,64]{2,3,1,0:T(8,128)} %fusion.2) | copy-start | bytes 4325380
  213.5 228.1 %all-reduce.2.cloned.1.call-start = ((), (), s32[]{:S(2)}) async-start(), calls=%async_computation.6 | async-start | bytes 262144 | tf_op jit(solution)/shard_map/psum | solution.py:92
  294.5 192.4 %copy-start.9 = (f32[4,64,128]{2,1,0:T(8,128)S(1)}, f32[4,64,128]{2,1,0:T(8,128)}, u32[]{:S(2)}) copy-start(f32[4,64,128]{2,1,0:T(8,128)} %reduce-scatter.5.cloned.1.call-done) | copy-start | bytes 393220
Sparse Core Ops, SparseCore 0:
  10.2 49.7 all-gather.2
  63.7 79.6 reduce-scatter.2
  146.2 47.5 all-gather.4
  213.6 79.7 reduce-scatter.4
  298.5 142.9 all-reduce.1
where the time goes:
time: 496 us; the launch traced here: 495 us
  waiting for transfers between devices  343 us (69%)
  other arithmetic  55.1 us (11%)
  matrix products  30.5 us (6%)
  local copies, waits for them, and re-layouts  28.1 us (6%)
  blocking collectives  23.2 us (5%)
  between operations  14.3 us (3%)
    psum x1, waiting for transfers between devices, local(): grams = lax.psum(grams, ('group', 'bulk'))  146 us
    reduce_scatter x1, waiting for transfers between devices, local(): u2 = lax.psum_scatter(buffer, 'bulk', scatter_dimension=0, tiled=True)  72.2 us
    reduce_scatter x1, waiting for transfers between devices, local(): u1 = own + lax.psum_scatter(buffer, 'bulk', scatter_dimension=0, tiled=True)  71 us
    all_gather x2, waiting for transfers between devices, off_part(): panel = lax.all_gather(vectors, 'bulk', axis=0, tiled=True)  52.9 us
    all_gather x2, blocking collectives, off_part(): lax.all_gather(vectors[:boundary_rows], 'group', axis=0, tiled=True)  23.2 us
    another operation x9, other arithmetic, chol_apply(): factor = jnp.linalg.cholesky(matrix)  19.6 us
    another operation x6, other arithmetic, chol_apply(): lax.linalg.triangular_solve(factor, middle, left_side=True, lower=True, t...  16.6 us
  transfers between devices with their start and end apart: 5, of which 5 were waited for; matrix products, arithmetic and copies ran while one was open for 9% of the time, Pallas kernels for 0%

commit v1 on v0

--- a/solution.py
+++ b/solution.py
@@ -5,6 +5,12 @@
 
 highest = lax.Precision.HIGHEST
 diagonal_shift = 4.0
+
+
+def supply_all_the_teams(frame_in, mesh_ax):
+    after = lax.axis_size(mesh_ax)
+    local_next = jnp.concatenate([frame_in] * after, 0)
+    return lax.all_to_all(local_next, mesh_ax, 0, 0, tiled=True)
 
 
 def chol_apply(matrix, right):
@@ -31,7 +37,7 @@
     border = lax.all_gather(vectors[:boundary_rows], "group", axis=0, tiled=True)
     own = jnp.einsum("rnj,rij->rni", vectors, diag, precision=highest)
     returned = jnp.einsum("rni,rkij->rknj", vectors, masked, precision=highest)
-    panel = lax.all_gather(vectors, "bulk", axis=0, tiled=True)
+    panel = supply_all_the_teams(vectors, "bulk")
     picked = panel[column_ids]
     own = own + jnp.einsum("rknj,rkij->rni", picked, masked, precision=highest)
     border = border.reshape((part_count, boundary_rows) + vectors.shape[1:])

time: 496 us -> 514 us (1.036)
  waiting for transfers between devices: 343 us -> 302 us
  local copies, waits for them, and re-layouts: 28.1 us -> 68.2 us
  starting transfers between devices: 0.2 us -> 17.3 us
    all_to_all x0 -> x2, waiting for transfers between devices: none -> 75.2 us  [supply_all_the_teams(): return lax.all_to_all(local_next, mesh_ax, 0, 0, tiled=True)]
    reduce_scatter x1, waiting for transfers between devices: 71 us -> 8.16 us  [local(): u1 = own + lax.psum_scatter(buffer, 'bulk', scatter_dimension=0, tiled=True)]
    all_gather x2 -> x0, waiting for transfers between devices: 52.9 us -> none  [off_part(): panel = lax.all_gather(vectors, 'bulk', axis=0, tiled=True)]
    unnamed x21 -> x80, local copies, waits for them, and re-layouts: 0.95 us -> 40.2 us
    all_to_all x0 -> x2, starting transfers between devices: none -> 17.2 us  [supply_all_the_teams(): return lax.all_to_all(local_next, mesh_ax, 0, 0, tiled=True)]
  transfers between devices with their start and end apart: 5 -> 5, of which waited for: 5 -> 5; matrix products, arithmetic and copies ran while one was open for 9% -> 10% of each run, Pallas kernels for 0% -> 0%
where the time goes in v1:
time: 514 us; the launch traced here: 512 us
  waiting for transfers between devices  302 us (59%)
  local copies, waits for them, and re-layouts  68.2 us (13%)
  other arithmetic  57.7 us (11%)
  matrix products  29.7 us (6%)
  blocking collectives  22.8 us (4%)
  starting transfers between devices  17.3 us (3%)
  between operations  14.3 us (3%)
    psum x1, waiting for transfers between devices, local(): grams = lax.psum(grams, ('group', 'bulk'))  146 us
    all_to_all x2, waiting for transfers between devices, supply_all_the_teams(): return lax.all_to_all(local_next, mesh_ax, 0, 0, tiled=True)  75.2 us
    reduce_scatter x1, waiting for transfers between devices, local(): u2 = lax.psum_scatter(buffer, 'bulk', scatter_dimension=0, tiled=True)  72.6 us
    unnamed x80, local copies, waits for them, and re-layouts  40.2 us
    all_gather x2, blocking collectives, off_part(): lax.all_gather(vectors[:boundary_rows], 'group', axis=0, tiled=True)  22.8 us
    another operation x9, other arithmetic, chol_apply(): factor = jnp.linalg.cholesky(matrix)  19.6 us
    all_to_all x2, starting transfers between devices, supply_all_the_teams(): return lax.all_to_all(local_next, mesh_ax, 0, 0, tiled=True)  17.2 us
    another operation x6, other arithmetic, chol_apply(): lax.linalg.triangular_solve(factor, middle, left_side=True, lower=True, t...  16.6 us
  transfers between devices with their start and end apart: 5, of which 5 were waited for; matrix products, arithmetic and copies ran while one was open for 10% of the time, Pallas kernels for 0%

profile of v1, /device:TPU:1, one launch (start us, length us, event | category | flops | bytes accessed | tf_op | source)
XLA Modules:
  0.0 512.4 jit_solution(33475403279514044)
XLA Ops:
  9.1 3.8 fusion.4
  12.9 2.5 broadcast.140.clone
  15.4 6.9 %scatter_fusion = f32[128,64,128]{2,1,0:T(8,128)} fusion(f32[128,64,128]{2,1,0:T(8,128)} %broadcast.140.clone, s32[44]{0:T(128)S(1)} %reshape.206, f32[44,64,128]{2,1,0:T(8,128)S(1)} %bitcast.248), kind=kCustom, calls=%fused_computation.6 | custom fusion | flops 360448 | bytes 4325552 | tf_op jit(solution)/shard_map/scatter-add | solution.py:88
  43.3 9.8 %all-to-all-start = ((f32[128,64,128]{2,1,0:T(8,128)}), f32[128,64,128]{2,1,0:T(8,128)}, u32[]{:S(2)}, u32[]{:S(2)}) async-start(f32[128,64,128]{2,1,0:T(8,128)} %constant_dynamic-update-slice_fusion), calls=%async_computation | async-start | bytes 8388608 | tf_op jit(solution)/shard_map/all_to_all | solution.py:13
  53.8 11.3 %all_gather.6 = f32[8,64,128]{2,1,0:T(8,128)} all-gather(f32[2,64,128]{2,1,0:T(8,128)S(1)} %slice-done), channel_id=1, replica_groups=mesh['group'=4,'bulk'=32] {'group'}, dimensions={0}, use_global_device_ids=true | all-gather | bytes 327680 | tf_op jit(solution)/shard_map/all_gather | solution.py:37
  66.0 44.3 %all-to-all-done = f32[128,64,128]{2,1,0:T(8,128)} async-done(((f32[128,64,128]{2,1,0:T(8,128)}), f32[128,64,128]{2,1,0:T(8,128)}, u32[]{:S(2)}, u32[]{:S(2)}) %all-to-all-start) | async-done | bytes 4194336 | tf_op jit(solution)/shard_map/all_to_all | solution.py:13
  110.3 3.9 gather_fusion.1
  114.2 4.8 fusion.12
  119.1 1.3 convolution_add_fusion.1
  120.4 2.1 fusion.21
  122.5 8.2 %reduce-scatter.3.cloned.1.call-done = f32[4,64,128]{2,1,0:T(8,128)} async-done(((f32[128,64,128]{2,1,0:T(8,128)}), f32[4,64,128]{2,1,0:T(8,128)}) %reduce-scatter.3.cloned.1.call-update) | async-done | bytes 131088 | tf_op jit(solution)/shard_map/reduce_scatter | solution.py:89
  130.6 1.6 constant_dynamic-update-slice_fusion.63
  152.7 7.4 %all-to-all-start.1 = ((f32[128,64,128]{2,1,0:T(8,128)}), f32[128,64,128]{2,1,0:T(8,128)}, u32[]{:S(2)}, u32[]{:S(2)}) async-start(f32[128,64,128]{2,1,0:T(8,128)} %constant_dynamic-update-slice_fusion.32), calls=%async_computation.2 | async-start | bytes 8388608 | tf_op jit(solution)/shard_map/all_to_all | solution.py:13
  163.3 1.3 gather_fusion.3
  165.3 11.5 %all_gather.7 = f32[8,64,128]{2,1,0:T(8,128)} all-gather(f32[2,64,128]{2,1,0:T(8,128)S(1)} %slice.102), channel_id=1, replica_groups=mesh['group'=4,'bulk'=32] {'group'}, dimensions={0}, use_global_device_ids=true | all-gather | bytes 327680 | tf_op jit(solution)/shard_map/all_gather | solution.py:37
  176.8 3.2 fusion.2
  179.9 30.8 %all-to-all-done.1 = f32[128,64,128]{2,1,0:T(8,128)} async-done(((f32[128,64,128]{2,1,0:T(8,128)}), f32[128,64,128]{2,1,0:T(8,128)}, u32[]{:S(2)}, u32[]{:S(2)}) %all-to-all-start.1) | async-done | bytes 4194336 | tf_op jit(solution)/shard_map/all_to_all | solution.py:13
  210.8 4.0 gather_fusion.4
  214.8 4.9 fusion.15
  221.2 2.5 broadcast.140
  223.7 6.9 %scatter_fusion.1 = f32[128,64,128]{2,1,0:T(8,128)} fusion(f32[128,64,128]{2,1,0:T(8,128)} %broadcast.140, s32[48]{0:T(128)S(1)} %pad_add_fusion, f32[48,64,128]{2,1,0:T(8,128)S(1)} %pad_maximum_fusion), kind=kCustom, calls=%fused_computation.7 | custom fusion | flops 393216 | bytes 4718784 | tf_op jit(solution)/shard_map/scatter-add | solution.py:92
  230.6 1.3 scatter_custom_fusion
  232.1 2.7 gather_fusion
  235.1 2.7 gather_fusion.2
  238.3 72.6 %reduce-scatter.5.cloned.1.call-done = f32[4,64,128]{2,1,0:T(8,128)} async-done(((f32[128,64,128]{2,1,0:T(8,128)}), f32[4,64,128]{2,1,0:T(8,128)}) %reduce-scatter.5.cloned.1.call-update) | async-done | bytes 131088 | tf_op jit(solution)/shard_map/reduce_scatter | solution.py:93
  312.9 146.4 %all-reduce.2.cloned.1.call-done = f32[4,64,64]{2,1,0:T(8,128)} async-done(((f32[4,64,64]{2,1,0:T(8,128)}), f32[4,64,64]{2,1,0:T(8,128)}) %all-reduce.2.cloned.1.call-update) | async-done | bytes 65552 | tf_op jit(solution)/shard_map/psum | solution.py:98
  461.3 5.9 %cholesky.59 = f32[64,64]{1,0:T(8,128)S(1)} custom-call(f32[64,64]{1,0:T(8,128)S(1)} %copy.82), custom_call_target="Cholesky" | custom-call | tf_op jit(solution)/shard_map/jit(cholesky)/cholesky | solution.py:17
  468.5 4.9 custom-call.13
  474.4 5.9 %cholesky.70 = f32[64,64]{1,0:T(8,128)S(1)} custom-call(f32[64,64]{1,0:T(8,128)S(1)} %copy.85), custom_call_target="Cholesky" | custom-call | tf_op jit(solution)/shard_map/jit(cholesky)/cholesky | solution.py:17
  481.7 4.9 custom-call.15
  491.6 5.8 %cholesky.81 = f32[64,64]{1,0:T(8,128)S(1)} custom-call(f32[64,64]{1,0:T(8,128)S(1)} %fusion.51), custom_call_target="Cholesky" | custom-call | tf_op jit(solution)/shard_map/jit(cholesky)/cholesky | solution.py:17
  498.8 4.9 custom-call.17
  (172 shorter events, 66.9 us)
Async XLA Ops:
  7.2 113.2 %copy-start = (f32[2,4,128,128]{3,2,1,0:T(8,128)S(1)}, f32[2,4,128,128]{3,2,1,0:T(8,128)}, u32[]{:S(2)}) copy-start(f32[2,4,128,128]{3,2,1,0:T(8,128)} %param.19) | copy-start | bytes 1572868
  7.2 123.5 %reduce-scatter.3.cloned.1.call-start = ((), (), s32[]{:S(2)}) async-start(), calls=%async_computation.4 | async-start | bytes 4325376 | tf_op jit(solution)/shard_map/reduce_scatter | solution.py:89
  15.4 6.9 %copy-start.1 = (f32[4,64,128]{2,1,0:T(8,128)S(1)}, f32[4,64,128]{2,1,0:T(8,128)}, u32[]{:S(2)}) copy-start(f32[4,64,128]{2,1,0:T(8,128)} %param.16) | copy-start | bytes 393220
  43.3 10.5 %slice-start = ((f32[4,64,128]{2,1,0:T(8,128)}), f32[2,64,128]{2,1,0:T(8,128)S(1)}, s32[]{:S(2)}) async-start(f32[4,64,128]{2,1,0:T(8,128)} %param.16), calls=%async_computation.7 | async-start | bytes 131072 | tf_op jit(solution)/shard_map/slice | solution.py:37
  43.3 67.0 %all-to-all-start = ((f32[128,64,128]{2,1,0:T(8,128)}), f32[128,64,128]{2,1,0:T(8,128)}, u32[]{:S(2)}, u32[]{:S(2)}) async-start(f32[128,64,128]{2,1,0:T(8,128)} %constant_dynamic-update-slice_fusion), calls=%async_computation | async-start | bytes 8388608 | tf_op jit(solution)/shard_map/all_to_all | solution.py:13
  65.2 49.1 %copy-start.2 = (f32[4,11,128,128]{3,2,1,0:T(8,128)S(1)}, f32[4,11,128,128]{3,2,1,0:T(8,128)}, u32[]{:S(2)}) copy-start(f32[4,11,128,128]{3,2,1,0:T(8,128)} %param.18) | copy-start | bytes 8650756
  114.2 4.9 copy-start.6
  114.2 6.1 %copy-start.5 = (f32[8,64,128]{2,1,0:T(8,128)S(1)}, f32[8,64,128]{2,1,0:T(8,128)}, u32[]{:S(2)}) copy-start(f32[8,64,128]{2,1,0:T(8,128)} %all_gather.6) | copy-start | bytes 786436
  152.7 58.1 %all-to-all-start.1 = ((f32[128,64,128]{2,1,0:T(8,128)}), f32[128,64,128]{2,1,0:T(8,128)}, u32[]{:S(2)}, u32[]{:S(2)}) async-start(f32[128,64,128]{2,1,0:T(8,128)} %constant_dynamic-update-slice_fusion.32), calls=%async_computation.2 | async-start | bytes 8388608 | tf_op jit(solution)/shard_map/all_to_all | solution.py:13
  160.1 150.9 %reduce-scatter.5.cloned.1.call-start = ((), (), s32[]{:S(2)}) async-start(), calls=%async_computation.5 | async-start | bytes 4325376 | tf_op jit(solution)/shard_map/reduce_scatter | solution.py:93
  214.8 4.9 copy-start.7
  214.8 5.6 %copy-start.4 = (f32[8,64,128]{2,1,0:T(8,128)S(1)}, f32[8,64,128]{2,1,0:T(8,128)}, u32[]{:S(2)}) copy-start(f32[8,64,128]{2,1,0:T(8,128)} %all_gather.7) | copy-start | bytes 786436
  214.8 6.2 %copy-start.3 = (f32[4,11,128,64]{2,3,1,0:T(8,128)S(1)}, f32[4,11,128,64]{2,3,1,0:T(8,128)}, u32[]{:S(2)}) copy-start(f32[4,11,128,64]{2,3,1,0:T(8,128)} %fusion.2) | copy-start | bytes 4325380
  230.6 228.7 %all-reduce.2.cloned.1.call-start = ((), (), s32[]{:S(2)}) async-start(), calls=%async_computation.6 | async-start | bytes 262144 | tf_op jit(solution)/shard_map/psum | solution.py:98
  311.0 193.7 %copy-start.8 = (f32[4,64,128]{2,1,0:T(8,128)S(1)}, f32[4,64,128]{2,1,0:T(8,128)}, u32[]{:S(2)}) copy-start(f32[4,64,128]{2,1,0:T(8,128)} %reduce-scatter.5.cloned.1.call-done) | copy-start | bytes 393220
Sparse Core Ops, SparseCore 0:
  22.4 108.2 reduce-scatter.2
  230.7 80.2 reduce-scatter.4
  316.3 142.9 all-reduce.1
